TPU v7x, 32 devices: a whole 2x2x4 slice. The times are simulated.
32 devices in a mesh: table: 2 (over x), batch: 16 (over z, y, core).
Axes of the slice: x: 2, y: 2, z: 4, core: 2. Of those that a mesh axis runs over, the one named last changes fastest.
Arguments:
- x_first: bfloat16 [2048, 4096], P('batch', 'table'), may hold values from -6 to 6
- x_layer: bfloat16 [2048, 4096], P('batch', 'table'), may hold values from -6 to 6
- pre_act: bfloat16 [2048, 4096], P('batch', 'table'), may hold values from -8 to 8
- gamma: float32 [4096], P('table'), may hold values from 0.3 to 3
- weight: float32 [4096, 4096], P('table', 'batch'), may hold values from -0.09375 to 0.09375
- cotangent: bfloat16 [2048, 4096], P('batch', 'table'), may hold values from -12 to 12
Outputs:
- grad_first: bfloat16 [2048, 4096], P('batch', 'table')
- grad_layer: bfloat16 [2048, 4096], P('batch', 'table')
- grad_weight: float32 [4096, 4096], P('table', 'batch')
- grad_bias: float32 [4096], P('table')
- grad_gamma: float32 [4096], P('table')
All inputs are finite; a program needn't handle non-finite values.
Results may differ from a plain program's by a relative error of at most 0.005.
Values may be sent and summed in bfloat16 or wider, within the bound.
A program may use at most 128 MiB of HBM per device.

v0:
```python
import jax
import jax.numpy as jnp
from jax import lax
from jax.sharding import PartitionSpec as P


def shards(x_first, x_layer, pre_act, gamma, weight, cotangent):
    weight_bf = weight.astype(jnp.bfloat16)
    pre_full = pre_act.astype(jnp.float32)
    gate_tanh = jnp.tanh(gamma[None, :] * pre_full)
    hidden = pre_full * gate_tanh
    cot_full = cotangent.astype(jnp.float32)
    grad_hidden = cot_full * x_first.astype(jnp.float32)
    grad_first = (cot_full * hidden).astype(jnp.bfloat16)
    slope = 1.0 - gate_tanh * gate_tanh
    grad_pre = (grad_hidden * (gate_tanh + gamma[None, :] * pre_full * slope)).astype(jnp.bfloat16)
    local_gamma = jnp.sum(grad_hidden * pre_full * pre_full * slope, axis=0)
    local_bias = jnp.sum(grad_pre.astype(jnp.float32), axis=0)
    grad_bias, grad_gamma = lax.psum((local_bias, local_gamma), "batch")
    layer_full = lax.all_gather(x_layer, "table", axis=1, tiled=True)
    layer_cols = lax.all_to_all(layer_full, "batch", split_axis=1, concat_axis=0, tiled=True)
    portion = lax.all_gather(grad_pre, "batch", axis=0, tiled=True)
    weight_sum = lax.dot_general(
        portion, layer_cols, (((0,), (0,)), ((), ())), preferred_element_type=jnp.float32
    )
    product = jnp.dot(portion, weight_bf, preferred_element_type=jnp.float32)
    input_part = product
    grad_weight, input_part = (weight_sum, input_part)
    returned = lax.all_to_all(input_part, "batch", split_axis=0, concat_axis=1, tiled=True)
    own_part = lax.psum_scatter(returned, "table", scatter_dimension=1, tiled=True)
    grad_layer = (cot_full + own_part).astype(jnp.bfloat16)
    return (grad_first, grad_layer, grad_weight, grad_bias, grad_gamma)


def solution(mesh):
    placed = (
        P("batch", "table"),
        P("batch", "table"),
        P("batch", "table"),
        P("table"),
        P("table", "batch"),
        P("batch", "table"),
    )
    return jax.shard_map(
        shards,
        mesh=mesh,
        in_specs=placed,
        out_specs=(
            P("batch", "table"),
            P("batch", "table"),
            P("table", "batch"),
            P("table"),
            P("table"),
        ),
        check_vma=False,
    )
```

profile of v0, /device:TPU:0, one launch (start us, length us, event | category | flops | bytes accessed | tf_op | source)
XLA Modules:
  0.0 244.0 jit_solution(13059168050492238537)
XLA Ops:
  8.0 0.0 copy-start.2
  8.0 0.0 all-gather.3.cloned.1.call-start
  8.1 3.2 %convert_reduce_fusion = (f32[2048]{0:T(1024)S(1)}, bf16[128,2048]{1,0:T(8,128)(2,1)}, f32[2048]{0:T(1024)S(1)}, bf16[128,2048]{1,0:T(8,128)(2,1)}) fusion(bf16[128,2048]{1,0:T(8,128)(2,1)} %param.8, f32[2048]{0:T(1024)} %param.9, bf16[128,2048]{1,0:T(8,128)(2,1)} %param.6, bf16[128,2048]{1,0:T(8,128)(2,1)} %param.11), kind=kLoop, calls=%fused_computation.18 | loop fusion | flops 5238784 | bytes 2646016 | tf_op jit(solution)/shard_map/reduce_sum | solution.py:18
  11.2 0.0 all-gather.3.cloned.1.call-update
  11.2 77.4 %all-gather.3.cloned.1.call-done = bf16[2048,2048]{1,0:T(8,128)(2,1)} async-done(((bf16[128,2048]{1,0:T(8,128)(2,1)}), bf16[2048,2048]{1,0:T(8,128)(2,1)}) %all-gather.3.cloned.1.call-update) | async-done | bytes 8388624 | tf_op jit(solution)/shard_map/all_gather | solution.py:22
  88.6 0.0 copy-done.2
  88.6 7.1 %fusion.11 = f32[2048,256]{1,0:T(8,128)} fusion(bf16[2048,2048]{1,0:T(8,128)(2,1)} %all-gather.3.cloned.1.call-done, f32[2048,256]{1,0:T(8,128)S(1)} %copy-done.2), kind=kOutput, calls=%fused_computation.19 | convolution fusion | flops 2148007936 | bytes 12582912 | tf_op jit(solution)/shard_map/dot_general | solution.py:26
  95.7 0.0 copy-start.1
  95.7 3.9 %all-to-all-start = ((f32[16,128,256]{2,1,0:T(8,128)}), f32[16,128,256]{2,1,0:T(8,128)S(1)}, u32[]{:S(2)}, u32[]{:S(2)}) async-start(f32[16,128,256]{2,1,0:T(8,128)} %bitcast.13), calls=%async_computation | async-start | bytes 4194304 | tf_op jit(solution)/shard_map/all_to_all | solution.py:29
  99.5 0.0 all-gather.5.cloned.1.call-start
  99.6 0.0 copy-done.1
  99.6 1.0 copy.14
  100.6 0.0 all-gather.5.cloned.1.call-update
  100.6 0.0 reduce-scatter.2.cloned.1.call-start
  100.7 39.8 %all-to-all-done = f32[16,128,256]{2,1,0:T(8,128)S(1)} async-done(((f32[16,128,256]{2,1,0:T(8,128)}), f32[16,128,256]{2,1,0:T(8,128)S(1)}, u32[]{:S(2)}, u32[]{:S(2)}) %all-to-all-start) | async-done | bytes 2097184 | tf_op jit(solution)/shard_map/all_to_all | solution.py:29
  140.4 1.6 copy.16
  142.0 0.0 reduce-scatter.2.cloned.1.call-update
  142.1 0.0 all-gather.5.cloned.1.call-done
  142.1 11.2 %all-to-all-start.1 = ((bf16[128,16,256]{0,2,1:T(8,128)(2,1)}), bf16[128,16,256]{0,2,1:T(8,128)(2,1)S(1)}, u32[]{:S(2)}, u32[]{:S(2)}) async-start(bf16[128,16,256]{0,2,1:T(8,128)(2,1)} %bitcast.14), calls=%async_computation.2 | async-start | bytes 2097152 | tf_op jit(solution)/shard_map/all_to_all | solution.py:21
  153.3 73.3 %all-reduce = (f32[2048]{0:T(1024)}, f32[2048]{0:T(1024)}) all-reduce(f32[2048]{0:T(1024)S(1)} %get-tuple-element.7, f32[2048]{0:T(1024)S(1)} %get-tuple-element.9), channel_id=1, replica_groups=mesh['table'=2,'batch'=16] {'batch'}, use_global_device_ids=true, to_apply=%region_2.0 | all-reduce | flops 4096 | bytes 32768 | tf_op jit(solution)/shard_map/psum | solution.py:19
  226.6 0.0 all-to-all-done.1
  226.6 0.5 copy.15
  227.2 0.0 copy-start
  227.2 7.2 %fusion.14 = f32[2048,256]{1,0:T(8,128)} fusion(bf16[2048,2048]{1,0:T(8,128)(2,1)} %all-gather.3.cloned.1.call-done, bf16[2048,256]{1,0:T(8,128)(2,1)S(1)} %bitcast.15), kind=kOutput, calls=%fused_computation.21 | convolution fusion | flops 2147483648 | bytes 11534336 | tf_op jit(solution)/shard_map/dot_general | solution.py:23
  234.4 0.0 reduce-scatter.2.cloned.1.call-done
  234.4 0.0 copy-done
  234.4 2.1 fusion.10
Async XLA Ops:
  8.0 80.6 %copy-start.2 = (f32[2048,256]{1,0:T(8,128)S(1)}, f32[2048,256]{1,0:T(8,128)}, u32[]{:S(2)}) copy-start(f32[2048,256]{1,0:T(8,128)} %param.10) | copy-start | bytes 6291460
  8.0 80.6 %all-gather.3.cloned.1.call-start = ((), (), s32[]{:S(2)}) async-start(), calls=%async_computation.3 | async-start | bytes 8912896 | tf_op jit(solution)/shard_map/all_gather | solution.py:22
  95.7 3.9 %copy-start.1 = (bf16[128,2048]{1,0:T(8,128)(2,1)S(1)}, bf16[128,2048]{1,0:T(8,128)(2,1)}, u32[]{:S(2)}) copy-start(bf16[128,2048]{1,0:T(8,128)(2,1)} %param.7) | copy-start | bytes 1572868
  95.7 44.8 %all-to-all-start = ((f32[16,128,256]{2,1,0:T(8,128)}), f32[16,128,256]{2,1,0:T(8,128)S(1)}, u32[]{:S(2)}, u32[]{:S(2)}) async-start(f32[16,128,256]{2,1,0:T(8,128)} %bitcast.13), calls=%async_computation | async-start | bytes 4194304 | tf_op jit(solution)/shard_map/all_to_all | solution.py:29
  99.5 42.6 %all-gather.5.cloned.1.call-start = ((), (), s32[]{:S(2)}) async-start(), calls=%async_computation.5 | async-start | bytes 1572864 | tf_op jit(solution)/shard_map/all_gather | solution.py:20
  100.6 133.8 %reduce-scatter.2.cloned.1.call-start = ((), (), s32[]{:S(2)}) async-start(), calls=%async_computation.4 | async-start | bytes 3145728 | tf_op jit(solution)/shard_map/reduce_scatter | solution.py:30
  142.1 84.5 %all-to-all-start.1 = ((bf16[128,16,256]{0,2,1:T(8,128)(2,1)}), bf16[128,16,256]{0,2,1:T(8,128)(2,1)S(1)}, u32[]{:S(2)}, u32[]{:S(2)}) async-start(bf16[128,16,256]{0,2,1:T(8,128)(2,1)} %bitcast.14), calls=%async_computation.2 | async-start | bytes 2097152 | tf_op jit(solution)/shard_map/all_to_all | solution.py:21
  227.2 7.2 %copy-start = (bf16[128,2048]{1,0:T(8,128)(2,1)S(1)}, bf16[128,2048]{1,0:T(8,128)(2,1)}, u32[]{:S(2)}) copy-start(bf16[128,2048]{1,0:T(8,128)(2,1)} %param.11) | copy-start | bytes 1572868
Sparse Core Ops, SparseCore 0:
  11.6 77.0 all-gather.2
Sparse Core Ops, SparseCore 1:
  102.1 22.4 all-gather.4
  142.1 38.3 reduce-scatter.1
where the time goes:
time: 244 us
  waiting for transfers between devices  117 us (48%)
  blocking collectives  73.3 us (30%)
  between operations  15.5 us (6%)
  starting transfers between devices  15.2 us (6%)
  matrix products  14.3 us (6%)
  other arithmetic  5.28 us (2%)
  local copies, waits for them, and re-layouts  3.12 us (1%)
    all_gather x1, waiting for transfers between devices, shards(): portion = lax.all_gather(grad_pre, 'batch', axis=0, tiled=True)  77.4 us
    psum x1, blocking collectives, shards(): grad_bias, grad_gamma = lax.psum((local_bias, local_gamma), 'batch')  73.3 us
    all_to_all x1, waiting for transfers between devices, shards(): lax.all_to_all(input_part, 'batch', split_axis=0, concat_axis=1, tiled=True)  39.8 us
    all_to_all x1, starting transfers between devices, shards(): lax.all_to_all(layer_full, 'batch', split_axis=1, concat_axis=0, tiled=True)  11.2 us
    dot_general x1, matrix products, shards(): lax.dot_general(portion, layer_cols, (((0,), (0,)), ((), ())), preferred_...  7.23 us
    dot_general x1, matrix products, shards(): product = jnp.dot(portion, weight_bf, preferred_element_type=jnp.float32)  7.05 us
  transfers between devices with their start and end apart: 5, of which 2 were waited for; matrix products, arithmetic and copies ran while one was open for 4% of the time, Pallas kernels for 0%

commit v1 on v0

v1 whole, which is shorter than its diff:
```python
import functools

import jax
import jax.numpy as jnp
from jax import lax
from jax.experimental import pallas as pl
from jax.experimental.pallas import tpu as pltpu
from jax.sharding import PartitionSpec as P

MESH = pl.DeviceIdType.MESH
F32 = jnp.float32
BF16 = jnp.bfloat16


def exchange(
    nt, nb, parts,
    pre_ref, cols_ref, weight_ref, small_ref,
    wsum_ref, ret_ref, total_ref,
    held, xall, shares, smalls, wfull, wbf,
    ring_send, ring_recv, sib_send, sib_recv, own_sem, x_send, x_recv,
    ret_send, ret_recv, small_send, small_recv, w_sem,
):
    rows, outs = pre_ref.shape
    per = nb // nt
    nc = nb // 2
    hops = nc // 2
    part = rows // parts
    t, b = lax.axis_index("table"), lax.axis_index("batch")
    q, c = b // 2, b % 2

    def chip_at(p):
        p = (p + nc) % nc
        return jnp.where(p < hops, 2 * p, 2 * (nc - 1 - p) + 1)

    p = jnp.where(q % 2 == 0, q // 2, nc - 1 - q // 2)
    ahead = [2 * chip_at(p + 1) + c, 2 * chip_at(p - 1) + c]
    origin = lambda d, k: chip_at(p - k if d == 0 else p + k)
    count = lambda d, core: jnp.where(core == d, hops, hops - 1)
    home = b // per
    slot = b % per

    def piece(chip, core, h):
        return held.at[chip, pl.ds(pl.multiple_of(core * rows + h * part, part), part), :]

    def block(ref, bb):
        return ref.at[bb // 2, pl.ds(pl.multiple_of((bb % 2) * rows, rows), rows), :]

    def done(ref, sem):
        pltpu.make_async_copy(ref, ref, sem).wait()

    def send(src, dst, ssem, rsem, tt, bb):
        return pltpu.make_async_remote_copy(
            src_ref=src, dst_ref=dst, send_sem=ssem, recv_sem=rsem, device_id=(tt, bb), device_id_type=MESH
        ).start()

    load_w = pltpu.make_async_copy(weight_ref, wfull, w_sem)
    load_w.start()
    barrier = pltpu.get_barrier_semaphore()

    def greet(i, carry):
        tt, bb = i // nb, i % nb

        @pl.when(jnp.logical_or(tt != t, bb != b))
        def _():
            pl.semaphore_signal(barrier, inc=1, device_id=(tt, bb), device_id_type=MESH)

        return carry

    lax.fori_loop(0, nt * nb, greet, 0)
    pl.semaphore_wait(barrier, nt * nb - 1)

    for h in range(parts):
        mine = pre_ref.at[pl.ds(h * part, part), :]
        for d in range(2):
            @pl.when(count(d, c) > 0)
            def _():
                send(mine, piece(q, c, h), ring_send.at[d, 0, h], ring_recv.at[d, 0, h], t, ahead[d])
    send(pre_ref, block(held, b), own_sem.at[0], own_sem.at[1], t, 2 * q + 1 - c)
    own_copy = pltpu.make_async_copy(pre_ref, block(held, b), own_sem.at[2])
    own_copy.start()

    def give_columns(i, carry):
        tt, j = i % nt, i // nt
        bb = t * per + j
        me = jnp.logical_and(tt == t, bb == b)

        @pl.when(me)
        def _():
            pltpu.make_async_copy(cols_ref.at[j], block(xall, b), x_recv.at[b]).start()

        @pl.when(jnp.logical_not(me))
        def _():
            send(cols_ref.at[j], block(xall, b), x_send.at[i], x_recv.at[b], tt, bb)

        return carry

    lax.fori_loop(0, nb, give_columns, 0)

    def give_small(bb, carry):
        @pl.when(bb != b)
        def _():
            send(small_ref, smalls.at[b], small_send.at[bb], small_recv.at[b], t, bb)

        return carry

    lax.fori_loop(0, nb, give_small, 0)
    load_w.wait()
    wbf[...] = wfull[...].astype(BF16)

    def product(chip):
        shares[chip] = jnp.dot(held[chip], wbf[...], preferred_element_type=F32).astype(BF16)

    def give_shares(chip):
        product(chip)
        for core in range(2):
            bb = 2 * chip + core
            send(block(shares, bb), ret_ref.at[t, slot], ret_send.at[bb], ret_recv.at[t, slot], home, bb)

    wide = 512 if outs % 512 == 0 else outs

    def add_weight(chip, first):
        for core in range(2):
            done(block(xall, 2 * chip + core), x_recv.at[2 * chip + core])

        def step(i, carry):
            at = pl.ds(pl.multiple_of(i * wide, wide), wide)
            term = lax.dot_general(
                held[chip, :, at], xall[chip], (((0,), (0,)), ((), ())), preferred_element_type=F32
            )
            wsum_ref[at, :] = term if first else wsum_ref[at, :] + term
            return carry

        lax.fori_loop(0, outs // wide, step, 0)

    own_copy.wait()
    done(block(held, b), own_sem.at[1])
    product(q)
    for core in range(2):
        bb = 2 * q + core
        me = jnp.logical_and(bb == b, home == t)

        @pl.when(me)
        def _():
            pltpu.make_async_copy(block(shares, bb), ret_ref.at[t, slot], ret_recv.at[t, slot]).start()

        @pl.when(jnp.logical_not(me))
        def _():
            send(block(shares, bb), ret_ref.at[t, slot], ret_send.at[bb], ret_recv.at[t, slot], home, bb)

    add_weight(q, True)

    def hop(k, carry):
        for h in range(parts):
            for d in range(2):
                here = piece(origin(d, k + 1), c, h)

                @pl.when(k < count(d, c))
                def _():
                    done(here, ring_recv.at[d, k, h])

                    @pl.when(k + 1 < count(d, c))
                    def _():
                        send(here, here, ring_send.at[d, k + 1, h], ring_recv.at[d, k + 1, h], t, ahead[d])

                    send(here, here, sib_send.at[d, k, h], sib_recv.at[d, k, h], t, 2 * q + 1 - c)
        for d in range(2):
            @pl.when(k < count(d, 1 - c))
            def _():
                for h in range(parts):
                    done(piece(origin(d, k + 1), 1 - c, h), sib_recv.at[d, k, h])
        give_shares(origin(0, k + 1))

        @pl.when(k < hops - 1)
        def _():
            give_shares(origin(1, k + 1))

        @pl.when(k > 0)
        def _():
            add_weight(origin(0, k), False)
            add_weight(origin(1, k), False)

        return carry

    lax.fori_loop(0, hops, hop, 0)
    add_weight(origin(0, hops), False)

    smalls[b] = small_ref[...]

    def take_small(bb, carry):
        @pl.when(bb != b)
        def _():
            done(smalls.at[bb], small_recv.at[bb])
            done(small_ref, small_send.at[bb])

        return carry

    lax.fori_loop(0, nb, take_small, 0)
    total_ref[...] = jnp.sum(smalls[...], axis=0)

    def sent_columns(i, carry):
        @pl.when(jnp.logical_or(i % nt != t, t * per + i // nt != b))
        def _():
            done(cols_ref.at[i // nt], x_send.at[i])

        return carry

    lax.fori_loop(0, nb, sent_columns, 0)

    def sent_shares(bb, carry):
        @pl.when(jnp.logical_or(bb != b, home != t))
        def _():
            done(block(shares, bb), ret_send.at[bb])

        done(ret_ref.at[bb // per, bb % per], ret_recv.at[bb // per, bb % per])
        return carry

    lax.fori_loop(0, nb, sent_shares, 0)
    done(pre_ref, own_sem.at[0])

    def sent_pieces(k, carry):
        for h in range(parts):
            for d in range(2):
                @pl.when(k < count(d, c))
                def _():
                    done(piece(origin(d, k), c, h), ring_send.at[d, k, h])
                    done(piece(origin(d, k + 1), c, h), sib_send.at[d, k, h])

        return carry

    lax.fori_loop(0, hops, sent_pieces, 0)


def run_exchange(nt, nb, grad_pre, columns, weight, small):
    rows, outs = grad_pre.shape
    cols = weight.shape[1]
    nc, per, hops = nb // 2, nb // nt, max(nb // 4, 1)
    parts = 4 if rows % 64 == 0 else 1
    dma = pltpu.SemaphoreType.DMA
    vmem = pl.BlockSpec(memory_space=pltpu.VMEM)
    return pl.pallas_call(
        functools.partial(exchange, nt, nb, parts),
        out_shape=(
            jax.ShapeDtypeStruct((outs, cols), F32),
            jax.ShapeDtypeStruct((nt, per, rows, cols), BF16),
            jax.ShapeDtypeStruct(small.shape, F32),
        ),
        in_specs=[vmem, vmem, pl.BlockSpec(memory_space=pl.ANY), vmem],
        out_specs=(vmem, vmem, vmem),
        scratch_shapes=[
            pltpu.VMEM((nc, 2 * rows, outs), BF16),
            pltpu.VMEM((nc, 2 * rows, cols), BF16),
            pltpu.VMEM((nc, 2 * rows, cols), BF16),
            pltpu.VMEM((nb,) + small.shape, F32),
            pltpu.VMEM((outs, cols), F32),
            pltpu.VMEM((outs, cols), BF16),
            dma((2, hops, parts)),
            dma((2, hops, parts)),
            dma((2, hops, parts)),
            dma((2, hops, parts)),
            dma((3,)),
            dma((nb,)),
            dma((nb,)),
            dma((nb,)),
            dma((nt, per)),
            dma((nb,)),
            dma((nb,)),
            dma,
        ],
        compiler_params=pltpu.CompilerParams(
            collective_id=0, has_side_effects=True, vmem_limit_bytes=60 * 1024 * 1024
        ),
    )(grad_pre, columns, weight, small)


def shards(nt, nb, x_first, x_layer, pre_act, gamma, weight, cotangent):
    pre_full = pre_act.astype(F32)
    gate_tanh = jnp.tanh(gamma[None, :] * pre_full)
    hidden = pre_full * gate_tanh
    cot_full = cotangent.astype(F32)
    grad_hidden = cot_full * x_first.astype(F32)
    grad_first = (cot_full * hidden).astype(BF16)
    slope = 1.0 - gate_tanh * gate_tanh
    grad_pre = (grad_hidden * (gate_tanh + gamma[None, :] * pre_full * slope)).astype(BF16)
    local_gamma = jnp.sum(grad_hidden * pre_full * pre_full * slope, axis=0)
    local_bias = jnp.sum(grad_pre.astype(F32), axis=0)
    small = jnp.stack([local_bias, local_gamma])
    rows = x_layer.shape[0]
    per = nb // nt
    columns = x_layer.reshape(rows, per, -1).transpose(1, 0, 2)
    grad_weight, returned, total = run_exchange(nt, nb, grad_pre, columns, weight, small)
    share = jnp.sum(returned.astype(F32), axis=0).transpose(1, 0, 2).reshape(rows, -1)
    grad_layer = (cot_full + share).astype(BF16)
    return (grad_first, grad_layer, grad_weight, total[0], total[1])


def solution(mesh):
    placed = (
        P("batch", "table"),
        P("batch", "table"),
        P("batch", "table"),
        P("table"),
        P("table", "batch"),
        P("batch", "table"),
    )
    return jax.shard_map(
        functools.partial(shards, mesh.shape["table"], mesh.shape["batch"]),
        mesh=mesh,
        in_specs=placed,
        out_specs=(
            P("batch", "table"),
            P("batch", "table"),
            P("table", "batch"),
            P("table"),
            P("table"),
        ),
        check_vma=False,
    )
```

time: 244 us -> 137 us (0.56)
  the two profiles are of different devices: /device:TPU:0 before, /device:TPU:14 now
where the time goes in v1:
time: 137 us; the launch traced here: 136 us
  Pallas kernels  126 us (92%)
  other arithmetic  4.66 us (3%)
  local copies, waits for them, and re-layouts  4.64 us (3%)
    pallas_call x1, Pallas kernels, run_exchange(): pl.pallas_call(functools.partial(exchange, nt, nb, parts), out_shape=(jax...  126 us
    unnamed x14, local copies, waits for them, and re-layouts  2.91 us

profile of v1, /device:TPU:14, one launch (start us, length us, event | category | flops | bytes accessed | tf_op | source)
XLA Modules:
  0.0 135.5 jit_solution(16248932150494094636)
XLA Ops:
  0.6 0.0 copy-start.1
  0.6 0.0 copy-start.5
  0.7 0.0 copy-start.2
  0.7 0.0 copy-start.3
  0.7 1.4 %copy.13 = bf16[128,2048]{0,1:T(8,128)(2,1)S(1)} copy(bf16[128,2048]{1,0:T(8,128)(2,1)} %param.7) | data formatting | bytes 1048576 | tf_op args[1]
  2.1 1.0 copy.14
  3.1 0.0 copy-done.1
  3.1 0.0 copy-done.5
  3.1 0.0 copy-done.2
  3.1 0.0 copy-done.3
  3.1 1.6 %convert_reduce_fusion.1 = (f32[2048]{0:T(1024)S(1)}, bf16[128,2048]{1,0:T(8,128)(2,1)}, f32[2048]{0:T(1024)S(1)}, bf16[128,2048]{1,0:T(8,128)(2,1)}) fusion(bf16[128,2048]{1,0:T(8,128)(2,1)S(1)} %copy-done.2, f32[2048]{0:T(1024)S(1)} %copy-done.5, bf16[128,2048]{1,0:T(8,128)(2,1)S(1)} %copy-done.3, bf16[128,2048]{1,0:T(8,128)(2,1)S(1)} %copy-done.1), kind=kLoop, calls=%fused_computation.19 | loop fusion | flops 5238784 | bytes 2646016 | tf_op jit(solution)/shard_map/reduce_sum | solution.py:285
  4.8 0.6 pad_maximum_fusion.small_ref
  5.4 125.5 %shard_map.101 = (f32[2048,256]{1,0:T(8,128)}, bf16[2,8,128,256]{3,2,1,0:T(8,128)(2,1)}, f32[2,2048]{1,0:T(2,128)}) custom-call(bf16[128,2048]{1,0:T(8,128)(2,1)} %get-tuple-element.12.pre_ref, bf16[8,128,256]{2,1,0:T(8,128)(2,1)} %bitcast.12, f32[2048,256]{1,0:T(8,128)} %weight_ref.1, f32[2,2048]{1,0:T(2,128)} %pad_maximum_fusion.small_ref), custom_call_target="tpu_custom_call" | custom-call | tf_op jit(solution)/shard_map/pallas_call | solution.py:240
  130.9 1.5 %convert_reduce_fusion = f32[8,128,256]{2,1,0:T(8,128)S(1)} fusion(bf16[2,8,128,256]{3,2,1,0:T(8,128)(2,1)} %get-tuple-element.8), kind=kLoop, calls=%fused_computation | loop fusion | flops 786432 | bytes 2097152 | tf_op jit(solution)/shard_map/reduce_sum | solution.py:291
  132.4 0.0 copy-start.4
  132.4 0.0 copy-start
  132.4 0.1 copy.16
  132.6 0.9 fusion.10
  133.5 0.0 copy-done.4
  133.5 0.6 fusion.12
  134.1 0.1 copy-done
  134.2 1.3 copy.18
Async XLA Ops:
  0.6 2.5 %copy-start.1 = (bf16[128,2048]{1,0:T(8,128)(2,1)S(1)}, bf16[128,2048]{1,0:T(8,128)(2,1)}, u32[]{:S(2)}) copy-start(bf16[128,2048]{1,0:T(8,128)(2,1)} %param.11) | copy-start | bytes 1572868
  0.6 2.5 %copy-start.5 = (f32[2048]{0:T(1024)S(1)}, f32[2048]{0:T(1024)}, u32[]{:S(2)}) copy-start(f32[2048]{0:T(1024)} %param.9) | copy-start | bytes 24580
  0.7 2.5 %copy-start.2 = (bf16[128,2048]{1,0:T(8,128)(2,1)S(1)}, bf16[128,2048]{1,0:T(8,128)(2,1)}, u32[]{:S(2)}) copy-start(bf16[128,2048]{1,0:T(8,128)(2,1)} %param.8) | copy-start | bytes 1572868
  0.7 2.5 %copy-start.3 = (bf16[128,2048]{1,0:T(8,128)(2,1)S(1)}, bf16[128,2048]{1,0:T(8,128)(2,1)}, u32[]{:S(2)}) copy-start(bf16[128,2048]{1,0:T(8,128)(2,1)} %param.6) | copy-start | bytes 1572868
  132.4 1.0 copy-start.4
  132.4 1.8 %copy-start = (f32[2048,256]{1,0:T(8,128)S(1)}, f32[2048,256]{1,0:T(8,128)}, u32[]{:S(2)}) copy-start(f32[2048,256]{1,0:T(8,128)} %get-tuple-element.24) | copy-start | bytes 6291460

commit v2 on v1

v2 whole, which is shorter than its diff:
```python
import functools

import jax
import jax.numpy as jnp
from jax import lax
from jax.experimental import pallas as pl
from jax.experimental.pallas import tpu as pltpu
from jax.sharding import PartitionSpec as P

MESH = pl.DeviceIdType.MESH
F32 = jnp.float32
BF16 = jnp.bfloat16


def exchange(
    nb, parts,
    pre_ref, cols_ref, weight_ref, small_ref,
    wsum_ref, ret_ref, total_ref,
    held, xall, mine, theirs, inbox, summed, layover, smalls, wfull, wbf,
    ring_send, ring_recv, sib_send, sib_recv, own_sem, x_send, x_on, x_recv,
    pair_send, pair_recv, sum_send, lay_recv, lay_send, ret_recv, small_send, small_recv, w_sem,
):
    rows, outs = pre_ref.shape
    per = nb // 2
    nc = nb // 2
    hops = nc // 2
    part = rows // parts
    t, b = lax.axis_index("table"), lax.axis_index("batch")
    q, c = b // 2, b % 2
    other = 1 - t

    def chip_at(p):
        p = (p + nc) % nc
        return jnp.where(p < hops, 2 * p, 2 * (nc - 1 - p) + 1)

    p = jnp.where(q % 2 == 0, q // 2, nc - 1 - q // 2)
    ahead = [2 * chip_at(p + 1) + c, 2 * chip_at(p - 1) + c]
    origin = lambda d, k: chip_at(p - k if d == 0 else p + k)
    count = lambda d, core: jnp.where(core == d, hops, hops - 1)
    home = b // per
    slot = b % per

    def piece(chip, core, h):
        return held.at[chip, pl.ds(pl.multiple_of(core * rows + h * part, part), part), :]

    def block(ref, bb):
        return ref.at[bb // 2, pl.ds(pl.multiple_of((bb % 2) * rows, rows), rows), :]

    def done(ref, sem):
        pltpu.make_async_copy(ref, ref, sem).wait()

    def send(src, dst, ssem, rsem, tt, bb):
        return pltpu.make_async_remote_copy(
            src_ref=src, dst_ref=dst, send_sem=ssem, recv_sem=rsem, device_id=(tt, bb), device_id_type=MESH
        ).start()

    def each(k, act):
        act(origin(0, k))

        @pl.when(jnp.logical_and(k > 0, k < hops))
        def _():
            act(origin(1, k))

    load_w = pltpu.make_async_copy(weight_ref, wfull, w_sem)
    load_w.start()
    barrier = pltpu.get_barrier_semaphore()

    def greet(i, carry):
        tt, bb = i // nb, i % nb

        @pl.when(jnp.logical_or(tt != t, bb != b))
        def _():
            pl.semaphore_signal(barrier, inc=1, device_id=(tt, bb), device_id_type=MESH)

        return carry

    lax.fori_loop(0, 2 * nb, greet, 0)
    pl.semaphore_wait(barrier, 2 * nb - 1)

    for h in range(parts):
        start = pre_ref.at[pl.ds(h * part, part), :]
        for d in range(2):
            @pl.when(count(d, c) > 0)
            def _():
                send(start, piece(q, c, h), ring_send.at[d, 0, h], ring_recv.at[d, 0, h], t, ahead[d])
    send(pre_ref, block(held, b), own_sem.at[0], own_sem.at[1], t, 2 * q + 1 - c)
    own_copy = pltpu.make_async_copy(pre_ref, block(held, b), own_sem.at[2])
    own_copy.start()

    first = (t + b) % 2

    def give_columns(j, carry):
        bb = t * per + (j + slot) % per
        me = jnp.logical_and(first == t, bb == b)
        own = cols_ref.at[(j + slot) % per]

        @pl.when(me)
        def _():
            pltpu.make_async_copy(own, block(xall, b), x_recv.at[b]).start()

        @pl.when(jnp.logical_not(me))
        def _():
            send(own, block(xall, b), x_send.at[j], x_recv.at[b], first, bb)

        return carry

    lax.fori_loop(0, per, give_columns, 0)

    def give_small(bb, carry):
        @pl.when(bb != b)
        def _():
            send(small_ref, smalls.at[b], small_send.at[bb], small_recv.at[b], t, bb)

        return carry

    lax.fori_loop(0, nb, give_small, 0)
    load_w.wait()
    wbf[...] = wfull[...].astype(BF16)
    wsum_ref[...] = jnp.zeros_like(wsum_ref)

    def lands_here(bb):
        return (home + bb) % 2 == t

    def pass_columns(chip):
        for core in range(2):
            bb = 2 * chip + core

            @pl.when(lands_here(bb))
            def _():
                done(block(xall, bb), x_recv.at[bb])
                send(block(xall, bb), block(xall, bb), x_on.at[bb], x_recv.at[bb], other, b)

    def half(chip, which):
        at = pl.ds(pl.multiple_of(which * rows, rows), rows)
        return jnp.dot(held[chip, at, :], wbf[...], preferred_element_type=F32)

    def multiply(chip):
        theirs[chip] = half(chip, other).astype(BF16)
        send(theirs.at[chip], inbox.at[chip], pair_send.at[chip], pair_recv.at[chip], other, b)
        mine[chip] = half(chip, t)

    def give_sum(chip):
        done(inbox.at[chip], pair_recv.at[chip])
        summed[chip] = (mine[chip] + inbox[chip].astype(F32)).astype(BF16)
        bb = 2 * chip + t
        for stays, dst, rsem in ((True, ret_ref, ret_recv), (False, layover, lay_recv)):
            right = (home == t) if stays else (home != t)

            @pl.when(jnp.logical_and(right, bb == b))
            def _():
                pltpu.make_async_copy(summed.at[chip], dst.at[slot], rsem.at[slot]).start()

            @pl.when(jnp.logical_and(right, bb != b))
            def _():
                send(summed.at[chip], dst.at[slot], sum_send.at[chip], rsem.at[slot], t, bb)

    def pass_sum(chip):
        for core in range(2):
            bb = 2 * chip + core
            j = bb % per

            @pl.when(jnp.logical_and(c == t, bb // per != t))
            def _():
                done(layover.at[j], lay_recv.at[j])
                send(layover.at[j], ret_ref.at[j], lay_send.at[j], ret_recv.at[j], other, b)

    wide = 512 if outs % 512 == 0 else outs

    def add_weight(chip):
        for core in range(2):
            bb = 2 * chip + core

            @pl.when(jnp.logical_not(lands_here(bb)))
            def _():
                done(block(xall, bb), x_recv.at[bb])

        def step(i, carry):
            at = pl.ds(pl.multiple_of(i * wide, wide), wide)
            wsum_ref[at, :] += lax.dot_general(
                held[chip, :, at], xall[chip], (((0,), (0,)), ((), ())), preferred_element_type=F32
            )
            return carry

        lax.fori_loop(0, outs // wide, step, 0)

    own_copy.wait()
    done(block(held, b), own_sem.at[1])
    multiply(q)
    pass_columns(q)

    def hop(k, carry):
        for h in range(parts):
            for d in range(2):
                here = piece(origin(d, k + 1), c, h)

                @pl.when(k < count(d, c))
                def _():
                    done(here, ring_recv.at[d, k, h])

                    @pl.when(k + 1 < count(d, c))
                    def _():
                        send(here, here, ring_send.at[d, k + 1, h], ring_recv.at[d, k + 1, h], t, ahead[d])

                    send(here, here, sib_send.at[d, k, h], sib_recv.at[d, k, h], t, 2 * q + 1 - c)
        each(k, give_sum)
        each(k + 1, pass_columns)
        for d in range(2):
            @pl.when(k < count(d, 1 - c))
            def _():
                for h in range(parts):
                    done(piece(origin(d, k + 1), 1 - c, h), sib_recv.at[d, k, h])
        each(k + 1, multiply)

        @pl.when(k > 0)
        def _():
            each(k - 1, pass_sum)

        each(k, add_weight)
        return carry

    lax.fori_loop(0, hops, hop, 0)
    each(hops, give_sum)
    each(hops - 1, pass_sum)
    each(hops, add_weight)
    each(hops, pass_sum)

    smalls[b] = small_ref[...]

    def take_small(bb, carry):
        @pl.when(bb != b)
        def _():
            done(smalls.at[bb], small_recv.at[bb])
            done(small_ref, small_send.at[bb])

        return carry

    lax.fori_loop(0, nb, take_small, 0)
    total_ref[...] = jnp.sum(smalls[...], axis=0)

    def sent_columns(j, carry):
        @pl.when(jnp.logical_or(first != t, t * per + (j + slot) % per != b))
        def _():
            done(cols_ref.at[j], x_send.at[j])

        return carry

    lax.fori_loop(0, per, sent_columns, 0)

    def sent_on(bb, carry):
        @pl.when(lands_here(bb))
        def _():
            done(block(xall, bb), x_on.at[bb])

        return carry

    lax.fori_loop(0, nb, sent_on, 0)

    def sent_sums(chip, carry):
        done(theirs.at[chip], pair_send.at[chip])

        @pl.when(2 * chip + t != b)
        def _():
            done(summed.at[chip], sum_send.at[chip])

        return carry

    lax.fori_loop(0, nc, sent_sums, 0)

    def came(j, carry):
        done(ret_ref.at[j], ret_recv.at[j])

        @pl.when(c == t)
        def _():
            done(layover.at[j], lay_send.at[j])

        return carry

    lax.fori_loop(0, per, came, 0)
    done(pre_ref, own_sem.at[0])

    def sent_pieces(k, carry):
        for h in range(parts):
            for d in range(2):
                @pl.when(k < count(d, c))
                def _():
                    done(piece(origin(d, k), c, h), ring_send.at[d, k, h])
                    done(piece(origin(d, k + 1), c, h), sib_send.at[d, k, h])

        return carry

    lax.fori_loop(0, hops, sent_pieces, 0)


def run_exchange(nb, grad_pre, columns, weight, small):
    rows, outs = grad_pre.shape
    cols = weight.shape[1]
    nc, per, hops = nb // 2, nb // 2, nb // 4
    parts = 4 if rows % 64 == 0 else 1
    dma = pltpu.SemaphoreType.DMA
    vmem = pl.BlockSpec(memory_space=pltpu.VMEM)
    return pl.pallas_call(
        functools.partial(exchange, nb, parts),
        out_shape=(
            jax.ShapeDtypeStruct((outs, cols), F32),
            jax.ShapeDtypeStruct((per, rows, cols), BF16),
            jax.ShapeDtypeStruct(small.shape, F32),
        ),
        in_specs=[vmem, vmem, pl.BlockSpec(memory_space=pl.ANY), vmem],
        out_specs=(vmem, vmem, vmem),
        scratch_shapes=[
            pltpu.VMEM((nc, 2 * rows, outs), BF16),
            pltpu.VMEM((nc, 2 * rows, cols), BF16),
            pltpu.VMEM((nc, rows, cols), F32),
            pltpu.VMEM((nc, rows, cols), BF16),
            pltpu.VMEM((nc, rows, cols), BF16),
            pltpu.VMEM((nc, rows, cols), BF16),
            pltpu.VMEM((per, rows, cols), BF16),
            pltpu.VMEM((nb,) + small.shape, F32),
            pltpu.VMEM((outs, cols), F32),
            pltpu.VMEM((outs, cols), BF16),
            dma((2, hops, parts)),
            dma((2, hops, parts)),
            dma((2, hops, parts)),
            dma((2, hops, parts)),
            dma((3,)),
            dma((per,)),
            dma((nb,)),
            dma((nb,)),
            dma((nc,)),
            dma((nc,)),
            dma((nc,)),
            dma((per,)),
            dma((per,)),
            dma((per,)),
            dma((nb,)),
            dma((nb,)),
            dma,
        ],
        compiler_params=pltpu.CompilerParams(
            collective_id=0, has_side_effects=True, vmem_limit_bytes=60 * 1024 * 1024
        ),
    )(grad_pre, columns, weight, small)


def shards(nb, x_first, x_layer, pre_act, gamma, weight, cotangent):
    pre_full = pre_act.astype(F32)
    gate_tanh = jnp.tanh(gamma[None, :] * pre_full)
    hidden = pre_full * gate_tanh
    cot_full = cotangent.astype(F32)
    grad_hidden = cot_full * x_first.astype(F32)
    grad_first = (cot_full * hidden).astype(BF16)
    slope = 1.0 - gate_tanh * gate_tanh
    grad_pre = (grad_hidden * (gate_tanh + gamma[None, :] * pre_full * slope)).astype(BF16)
    local_gamma = jnp.sum(grad_hidden * pre_full * pre_full * slope, axis=0)
    local_bias = jnp.sum(grad_pre.astype(F32), axis=0)
    small = jnp.stack([local_bias, local_gamma])
    rows = x_layer.shape[0]
    per = nb // 2
    columns = x_layer.reshape(rows, per, -1).transpose(1, 0, 2)
    grad_weight, returned, total = run_exchange(nb, grad_pre, columns, weight, small)
    share = returned.astype(F32).transpose(1, 0, 2).reshape(rows, -1)
    grad_layer = (cot_full + share).astype(BF16)
    return (grad_first, grad_layer, grad_weight, total[0], total[1])


def solution(mesh):
    assert mesh.shape["table"] == 2 and mesh.shape["batch"] % 4 == 0
    placed = (
        P("batch", "table"),
        P("batch", "table"),
        P("batch", "table"),
        P("table"),
        P("table", "batch"),
        P("batch", "table"),
    )
    return jax.shard_map(
        functools.partial(shards, mesh.shape["batch"]),
        mesh=mesh,
        in_specs=placed,
        out_specs=(
            P("batch", "table"),
            P("batch", "table"),
            P("table", "batch"),
            P("table"),
            P("table"),
        ),
        check_vma=False,
    )
```

time: 137 us -> 110 us (0.80)
  Pallas kernels: 126 us -> 98.4 us
  local copies, waits for them, and re-layouts: 4.64 us -> 6.04 us
    pallas_call x1, Pallas kernels: 126 us -> 98.4 us  [run_exchange(): pl.pallas_call(functools.partial(exchange, nb, parts), out_shape=(jax.Sha...]
    reduce_sum x1 -> x0, other arithmetic: 1.5 us -> none  [shards(): jnp.sum(returned.astype(F32), axis=0).transpose(1, 0, 2).reshape(rows, -1)]
    unnamed x14 -> x12, local copies, waits for them, and re-layouts: 2.91 us -> 3.51 us
where the time goes in v2:
time: 110 us; the launch traced here: 109 us
  Pallas kernels  98.4 us (89%)
  local copies, waits for them, and re-layouts  6.04 us (5%)
  other arithmetic  4.29 us (4%)
    pallas_call x1, Pallas kernels, run_exchange(): pl.pallas_call(functools.partial(exchange, nb, parts), out_shape=(jax.Sha...  98.4 us
    unnamed x12, local copies, waits for them, and re-layouts  3.51 us

profile of v2, /device:TPU:14, one launch (start us, length us, event | category | flops | bytes accessed | tf_op | source)
XLA Modules:
  0.0 109.5 jit_solution(7946296497763978892)
XLA Ops:
  0.6 0.0 copy-start.1
  0.6 0.0 copy-start.4
  0.7 0.0 copy-start.2
  0.7 0.0 copy-start.3
  0.7 1.4 %copy.12 = bf16[128,2048]{0,1:T(8,128)(2,1)S(1)} copy(bf16[128,2048]{1,0:T(8,128)(2,1)} %param.7) | data formatting | bytes 1048576 | tf_op args[1]
  2.1 1.0 copy.13
  3.1 0.0 copy-done.1
  3.1 0.0 copy-done.4
  3.1 0.0 copy-done.2
  3.1 0.0 copy-done.3
  3.1 1.6 %convert_reduce_fusion = (f32[2048]{0:T(1024)S(1)}, bf16[128,2048]{1,0:T(8,128)(2,1)}, f32[2048]{0:T(1024)S(1)}, bf16[128,2048]{1,0:T(8,128)(2,1)}) fusion(bf16[128,2048]{1,0:T(8,128)(2,1)S(1)} %copy-done.2, f32[2048]{0:T(1024)S(1)} %copy-done.4, bf16[128,2048]{1,0:T(8,128)(2,1)S(1)} %copy-done.3, bf16[128,2048]{1,0:T(8,128)(2,1)S(1)} %copy-done.1), kind=kLoop, calls=%fused_computation.19 | loop fusion | flops 5238784 | bytes 2646016 | tf_op jit(solution)/shard_map/reduce_sum | solution.py:355
  4.8 0.6 pad_maximum_fusion.small_ref
  5.4 98.4 %shard_map.101 = (f32[2048,256]{1,0:T(8,128)}, bf16[8,128,256]{2,1,0:T(8,128)(2,1)}, f32[2,2048]{1,0:T(2,128)}) custom-call(bf16[128,2048]{1,0:T(8,128)(2,1)} %get-tuple-element.12.pre_ref, bf16[8,128,256]{2,1,0:T(8,128)(2,1)} %bitcast.12, f32[2048,256]{1,0:T(8,128)} %weight_ref.1, f32[2,2048]{1,0:T(2,128)} %pad_maximum_fusion.small_ref), custom_call_target="tpu_custom_call" | custom-call | tf_op jit(solution)/shard_map/pallas_call | solution.py:301
  103.8 1.4 %fusion.12 = (f32[1,2048]{1,0:T(1,128)}, f32[1,2048]{1,0:T(1,128)}) fusion(f32[2,2048]{1,0:T(2,128)} %get-tuple-element.10), kind=kLoop, calls=%fused_computation.21 | loop fusion | bytes 32768 | tf_op jit(solution)/shard_map/slice | solution.py:363
  105.2 1.1 %convert_bitcast_fusion = f32[8,16,8,256]{3,2,1,0:T(8,128)S(1)} fusion(bf16[8,128,256]{2,1,0:T(8,128)(2,1)} %get-tuple-element.8), kind=kLoop, calls=%fused_computation.18 | loop fusion | flops 262144 | bytes 1572864
  106.4 0.0 copy-start
  106.4 0.1 copy.15
  106.5 0.9 fusion.10
  107.4 0.8 copy-done
  108.2 1.3 %copy.17 = f32[2048,256]{1,0:T(8,128)} copy(f32[2048,256]{1,0:T(8,128)S(1)} %copy-done) | data formatting | bytes 4194304
Async XLA Ops:
  0.6 2.5 %copy-start.1 = (bf16[128,2048]{1,0:T(8,128)(2,1)S(1)}, bf16[128,2048]{1,0:T(8,128)(2,1)}, u32[]{:S(2)}) copy-start(bf16[128,2048]{1,0:T(8,128)(2,1)} %param.11) | copy-start | bytes 1572868
  0.6 2.5 %copy-start.4 = (f32[2048]{0:T(1024)S(1)}, f32[2048]{0:T(1024)}, u32[]{:S(2)}) copy-start(f32[2048]{0:T(1024)} %param.9) | copy-start | bytes 24580
  0.7 2.5 %copy-start.2 = (bf16[128,2048]{1,0:T(8,128)(2,1)S(1)}, bf16[128,2048]{1,0:T(8,128)(2,1)}, u32[]{:S(2)}) copy-start(bf16[128,2048]{1,0:T(8,128)(2,1)} %param.8) | copy-start | bytes 1572868
  0.7 2.5 %copy-start.3 = (bf16[128,2048]{1,0:T(8,128)(2,1)S(1)}, bf16[128,2048]{1,0:T(8,128)(2,1)}, u32[]{:S(2)}) copy-start(bf16[128,2048]{1,0:T(8,128)(2,1)} %param.6) | copy-start | bytes 1572868
  106.4 1.8 %copy-start = (f32[2048,256]{1,0:T(8,128)S(1)}, f32[2048,256]{1,0:T(8,128)}, u32[]{:S(2)}) copy-start(f32[2048,256]{1,0:T(8,128)} %get-tuple-element.24) | copy-start | bytes 6291460

commit v3 on v2

--- a/solution.py
+++ b/solution.py
@@ -14,10 +14,10 @@
 
 def exchange(
     nb, parts,
-    pre_ref, cols_ref, weight_ref, small_ref,
+    pre_ref, cols_ref, weight_ref, bias_ref, gamma_ref,
     wsum_ref, ret_ref, total_ref,
-    held, xall, mine, theirs, inbox, summed, layover, smalls, wfull, wbf,
-    ring_send, ring_recv, sib_send, sib_recv, own_sem, x_send, x_on, x_recv,
+    held, xall, mine, theirs, inbox, summed, layover, guest, small_ref, smalls, wfull, wbf,
+    ring_send, ring_recv, sib_send, sib_recv, own_sem, x_send, x_on, x_recv, swap,
     pair_send, pair_recv, sum_send, lay_recv, lay_send, ret_recv, small_send, small_recv, w_sem,
 ):
     rows, outs = pre_ref.shape
@@ -46,6 +46,10 @@
     def block(ref, bb):
         return ref.at[bb // 2, pl.ds(pl.multiple_of((bb % 2) * rows, rows), rows), :]
 
+    def features(ref, j):
+        cols = wfull.shape[1]
+        return ref.at[j] if len(ref.shape) == 3 else ref.at[:, pl.ds(pl.multiple_of(j * cols, cols), cols)]
+
     def done(ref, sem):
         pltpu.make_async_copy(ref, ref, sem).wait()
 
@@ -63,6 +67,8 @@
 
     load_w = pltpu.make_async_copy(weight_ref, wfull, w_sem)
     load_w.start()
+    small_ref[0:1, :] = bias_ref[...]
+    small_ref[1:2, :] = gamma_ref[...]
     barrier = pltpu.get_barrier_semaphore()
 
     def greet(i, carry):
@@ -87,24 +93,33 @@
     own_copy = pltpu.make_async_copy(pre_ref, block(held, b), own_sem.at[2])
     own_copy.start()
 
-    first = (t + b) % 2
-
-    def give_columns(j, carry):
-        bb = t * per + (j + slot) % per
-        me = jnp.logical_and(first == t, bb == b)
-        own = cols_ref.at[(j + slot) % per]
-
-        @pl.when(me)
-        def _():
-            pltpu.make_async_copy(own, block(xall, b), x_recv.at[b]).start()
-
-        @pl.when(jnp.logical_not(me))
-        def _():
-            send(own, block(xall, b), x_send.at[j], x_recv.at[b], first, bb)
-
-        return carry
-
-    lax.fori_loop(0, per, give_columns, 0)
+    odd = b % 2 == 1
+    side = jnp.where(odd, other, t)
+
+    def give_columns(source):
+        def give(j, carry):
+            at = (j + slot) % per
+            bb = side * per + at
+
+            @pl.when(bb == b)
+            def _():
+                pltpu.make_async_copy(features(source, at), block(xall, b), x_recv.at[b]).start()
+
+            @pl.when(bb != b)
+            def _():
+                send(features(source, at), block(xall, b), x_send.at[at], x_recv.at[b], t, bb)
+
+            return carry
+
+        lax.fori_loop(0, per, give, 0)
+
+    @pl.when(odd)
+    def _():
+        send(cols_ref, guest, swap.at[0], swap.at[1], other, b)
+
+    @pl.when(jnp.logical_not(odd))
+    def _():
+        give_columns(cols_ref)
 
     def give_small(bb, carry):
         @pl.when(bb != b)
@@ -148,11 +163,11 @@
 
             @pl.when(jnp.logical_and(right, bb == b))
             def _():
-                pltpu.make_async_copy(summed.at[chip], dst.at[slot], rsem.at[slot]).start()
+                pltpu.make_async_copy(summed.at[chip], features(dst, slot), rsem.at[slot]).start()
 
             @pl.when(jnp.logical_and(right, bb != b))
             def _():
-                send(summed.at[chip], dst.at[slot], sum_send.at[chip], rsem.at[slot], t, bb)
+                send(summed.at[chip], features(dst, slot), sum_send.at[chip], rsem.at[slot], t, bb)
 
     def pass_sum(chip):
         for core in range(2):
@@ -162,7 +177,7 @@
             @pl.when(jnp.logical_and(c == t, bb // per != t))
             def _():
                 done(layover.at[j], lay_recv.at[j])
-                send(layover.at[j], ret_ref.at[j], lay_send.at[j], ret_recv.at[j], other, b)
+                send(layover.at[j], features(ret_ref, j), lay_send.at[j], ret_recv.at[j], other, b)
 
     wide = 512 if outs % 512 == 0 else outs
 
@@ -186,6 +201,12 @@
     own_copy.wait()
     done(block(held, b), own_sem.at[1])
     multiply(q)
+
+    @pl.when(odd)
+    def _():
+        done(guest, swap.at[1])
+        give_columns(guest)
+
     pass_columns(q)
 
     def hop(k, carry):
@@ -237,10 +258,14 @@
     lax.fori_loop(0, nb, take_small, 0)
     total_ref[...] = jnp.sum(smalls[...], axis=0)
 
+    @pl.when(odd)
+    def _():
+        done(cols_ref, swap.at[0])
+
     def sent_columns(j, carry):
-        @pl.when(jnp.logical_or(first != t, t * per + (j + slot) % per != b))
-        def _():
-            done(cols_ref.at[j], x_send.at[j])
+        @pl.when(side * per + j != b)
+        def _():
+            done(features(cols_ref, j), x_send.at[j])
 
         return carry
 
@@ -267,7 +292,7 @@
     lax.fori_loop(0, nc, sent_sums, 0)
 
     def came(j, carry):
-        done(ret_ref.at[j], ret_recv.at[j])
+        done(features(ret_ref, j), ret_recv.at[j])
 
         @pl.when(c == t)
         def _():
@@ -291,7 +316,7 @@
     lax.fori_loop(0, hops, sent_pieces, 0)
 
 
-def run_exchange(nb, grad_pre, columns, weight, small):
+def run_exchange(nb, grad_pre, columns, weight, bias, gamma):
     rows, outs = grad_pre.shape
     cols = weight.shape[1]
     nc, per, hops = nb // 2, nb // 2, nb // 4
@@ -302,10 +327,10 @@
         functools.partial(exchange, nb, parts),
         out_shape=(
             jax.ShapeDtypeStruct((outs, cols), F32),
-            jax.ShapeDtypeStruct((per, rows, cols), BF16),
-            jax.ShapeDtypeStruct(small.shape, F32),
+            jax.ShapeDtypeStruct(columns.shape, BF16),
+            jax.ShapeDtypeStruct((2, outs), F32),
         ),
-        in_specs=[vmem, vmem, pl.BlockSpec(memory_space=pl.ANY), vmem],
+        in_specs=[vmem, vmem, pl.BlockSpec(memory_space=pl.ANY), vmem, vmem],
         out_specs=(vmem, vmem, vmem),
         scratch_shapes=[
             pltpu.VMEM((nc, 2 * rows, outs), BF16),
@@ -315,7 +340,9 @@
             pltpu.VMEM((nc, rows, cols), BF16),
             pltpu.VMEM((nc, rows, cols), BF16),
             pltpu.VMEM((per, rows, cols), BF16),
-            pltpu.VMEM((nb,) + small.shape, F32),
+            pltpu.VMEM(columns.shape, BF16),
+            pltpu.VMEM((2, outs), F32),
+            pltpu.VMEM((nb, 2, outs), F32),
             pltpu.VMEM((outs, cols), F32),
             pltpu.VMEM((outs, cols), BF16),
             dma((2, hops, parts)),
@@ -326,6 +353,7 @@
             dma((per,)),
             dma((nb,)),
             dma((nb,)),
+            dma((2,)),
             dma((nc,)),
             dma((nc,)),
             dma((nc,)),
@@ -339,7 +367,7 @@
         compiler_params=pltpu.CompilerParams(
             collective_id=0, has_side_effects=True, vmem_limit_bytes=60 * 1024 * 1024
         ),
-    )(grad_pre, columns, weight, small)
+    )(grad_pre, columns, weight, bias, gamma)
 
 
 def shards(nb, x_first, x_layer, pre_act, gamma, weight, cotangent):
@@ -353,13 +381,14 @@
     grad_pre = (grad_hidden * (gate_tanh + gamma[None, :] * pre_full * slope)).astype(BF16)
     local_gamma = jnp.sum(grad_hidden * pre_full * pre_full * slope, axis=0)
     local_bias = jnp.sum(grad_pre.astype(F32), axis=0)
-    small = jnp.stack([local_bias, local_gamma])
     rows = x_layer.shape[0]
-    per = nb // 2
-    columns = x_layer.reshape(rows, per, -1).transpose(1, 0, 2)
-    grad_weight, returned, total = run_exchange(nb, grad_pre, columns, weight, small)
-    share = returned.astype(F32).transpose(1, 0, 2).reshape(rows, -1)
-    grad_layer = (cot_full + share).astype(BF16)
+    per, cols = nb // 2, weight.shape[1]
+    aligned = cols % 128 == 0
+    columns = x_layer if aligned else x_layer.reshape(rows, per, cols).transpose(1, 0, 2)
+    grad_weight, share, total = run_exchange(nb, grad_pre, columns, weight, local_bias[None], local_gamma[None])
+    if not aligned:
+        share = share.transpose(1, 0, 2).reshape(rows, per * cols)
+    grad_layer = (cot_full + share.astype(F32)).astype(BF16)
     return (grad_first, grad_layer, grad_weight, total[0], total[1])
 
 

time: 110 us -> 98.6 us (0.90)
  Pallas kernels: 98.4 us -> 87.6 us
  local copies, waits for them, and re-layouts: 6.04 us -> 4.45 us
  other arithmetic: 4.29 us -> 5.58 us
    pallas_call x1, Pallas kernels: 98.4 us -> 87.6 us  [run_exchange(): pl.pallas_call(functools.partial(exchange, nb, parts), out_shape=(jax.Sha...]
    reduce_sum x1, other arithmetic: 1.64 us -> 3.62 us  [shards(): local_bias = jnp.sum(grad_pre.astype(F32), axis=0)]
    unnamed x1 -> x0, other arithmetic: 1.13 us -> none
    reshape x2 -> x0, local copies, waits for them, and re-layouts: 1.12 us -> none  [the longest x1 1.01 us: shards(): columns = x_layer.reshape(rows, per, -1).transpose(1, 0, 2)]
    unnamed x12 -> x3, local copies, waits for them, and re-layouts: 3.51 us -> 3.05 us
where the time goes in v3:
time: 98.6 us; the launch traced here: 98.3 us
  Pallas kernels  87.6 us (89%)
  other arithmetic  5.58 us (6%)
  local copies, waits for them, and re-layouts  4.45 us (5%)
    pallas_call x1, Pallas kernels, run_exchange(): pl.pallas_call(functools.partial(exchange, nb, parts), out_shape=(jax.Sha...  87.6 us
    reduce_sum x1, other arithmetic, shards(): local_bias = jnp.sum(grad_pre.astype(F32), axis=0)  3.62 us
    unnamed x3, local copies, waits for them, and re-layouts  3.05 us

profile of v3, /device:TPU:14, one launch (start us, length us, event | category | flops | bytes accessed | tf_op | source)
XLA Modules:
  0.0 98.3 jit_solution(13661408660368673081)
XLA Ops:
  0.6 3.6 %convert_reduce_fusion = (f32[2048]{0:T(1024)}, bf16[128,2048]{1,0:T(8,128)(2,1)}, f32[2048]{0:T(1024)}, bf16[128,2048]{1,0:T(8,128)(2,1)}) fusion(bf16[128,2048]{1,0:T(8,128)(2,1)} %param.8, f32[2048]{0:T(1024)} %param.9, bf16[128,2048]{1,0:T(8,128)(2,1)} %param.6, bf16[128,2048]{1,0:T(8,128)(2,1)} %param.11), kind=kLoop, calls=%fused_computation.18 | loop fusion | flops 5238784 | bytes 2646016 | tf_op jit(solution)/shard_map/reduce_sum | solution.py:383
  4.3 0.0 copy-start
  4.3 87.6 %shard_map.101 = (f32[2048,256]{1,0:T(8,128)}, bf16[128,2048]{1,0:T(8,128)(2,1)}, f32[2,2048]{1,0:T(2,128)}) custom-call(bf16[128,2048]{1,0:T(8,128)(2,1)} %get-tuple-element.12.pre_ref, bf16[128,2048]{1,0:T(8,128)(2,1)} %cols_ref.1, f32[2048,256]{1,0:T(8,128)} %weight_ref.1, f32[1,2048]{1,0:T(1,128)} %bitcast.4, f32[1,2048]{1,0:T(1,128)} %bitcast.5), custom_call_target="tpu_custom_call" | custom-call | tf_op jit(solution)/shard_map/pallas_call | solution.py:326
  91.9 0.0 copy-done
  91.9 2.0 %fusion.10 = bf16[128,2048]{1,0:T(8,128)(2,1)} fusion(bf16[128,2048]{1,0:T(8,128)(2,1)S(1)} %copy-done, bf16[128,2048]{1,0:T(8,128)(2,1)} %get-tuple-element.8), kind=kLoop, calls=%fused_computation.17 | loop fusion | flops 1048576 | bytes 1572864 | tf_op jit(solution)/shard_map/convert_element_type | solution.py:391
  93.9 1.4 %fusion.12 = (f32[1,2048]{1,0:T(1,128)}, f32[1,2048]{1,0:T(1,128)}) fusion(f32[2,2048]{1,0:T(2,128)} %get-tuple-element.10), kind=kLoop, calls=%fused_computation.19 | loop fusion | bytes 32768 | tf_op jit(solution)/shard_map/slice | solution.py:392
  95.3 3.0 %copy.12 = f32[2048,256]{1,0:T(8,128)} copy(f32[2048,256]{1,0:T(8,128)} %get-tuple-element.24) | data formatting | bytes 4194304
Async XLA Ops:
  4.3 87.6 %copy-start = (bf16[128,2048]{1,0:T(8,128)(2,1)S(1)}, bf16[128,2048]{1,0:T(8,128)(2,1)}, u32[]{:S(2)}) copy-start(bf16[128,2048]{1,0:T(8,128)(2,1)} %param.11) | copy-start | bytes 1572868

commit v4 on v3

--- a/solution.py
+++ b/solution.py
@@ -14,13 +14,13 @@
 
 def exchange(
     nb, parts,
-    pre_ref, cols_ref, weight_ref, bias_ref, gamma_ref,
-    wsum_ref, ret_ref, total_ref,
-    held, xall, mine, theirs, inbox, summed, layover, guest, small_ref, smalls, wfull, wbf,
+    x_ref, act_ref, cot_ref, gamma_ref, cols_ref, weight_ref,
+    first_ref, wsum_ref, ret_ref, total_ref,
+    pre_ref, held, xall, mine, theirs, inbox, summed, layover, guest, small_ref, smalls, wfull, wbf,
     ring_send, ring_recv, sib_send, sib_recv, own_sem, x_send, x_on, x_recv, swap,
     pair_send, pair_recv, sum_send, lay_recv, lay_send, ret_recv, small_send, small_recv, w_sem,
 ):
-    rows, outs = pre_ref.shape
+    rows, outs = x_ref.shape
     per = nb // 2
     nc = nb // 2
     hops = nc // 2
@@ -67,8 +67,6 @@
 
     load_w = pltpu.make_async_copy(weight_ref, wfull, w_sem)
     load_w.start()
-    small_ref[0:1, :] = bias_ref[...]
-    small_ref[1:2, :] = gamma_ref[...]
     barrier = pltpu.get_barrier_semaphore()
 
     def greet(i, carry):
@@ -81,6 +79,27 @@
         return carry
 
     lax.fori_loop(0, 2 * nb, greet, 0)
+    small_ref[...] = jnp.zeros_like(small_ref)
+    wide = 512 if outs % 512 == 0 else outs
+
+    def gate(i, carry):
+        at = pl.ds(pl.multiple_of(i * part, part), part)
+        for lane in range(0, outs, wide):
+            to = pl.ds(lane, wide)
+            sharp = gamma_ref[:, to]
+            act = act_ref[at, to].astype(F32)
+            cot = cot_ref[at, to].astype(F32)
+            tanh = jnp.tanh(sharp * act)
+            hidden = cot * x_ref[at, to].astype(F32)
+            slope = 1.0 - tanh * tanh
+            first_ref[at, to] = (cot * (act * tanh)).astype(BF16)
+            pre = (hidden * (tanh + sharp * act * slope)).astype(BF16)
+            pre_ref[at, to] = pre
+            small_ref[0:1, to] += jnp.sum(pre.astype(F32), axis=0, keepdims=True)
+            small_ref[1:2, to] += jnp.sum(hidden * act * act * slope, axis=0, keepdims=True)
+        return carry
+
+    lax.fori_loop(0, parts, gate, 0)
     pl.semaphore_wait(barrier, 2 * nb - 1)
 
     for h in range(parts):
@@ -178,8 +197,6 @@
             def _():
                 done(layover.at[j], lay_recv.at[j])
                 send(layover.at[j], features(ret_ref, j), lay_send.at[j], ret_recv.at[j], other, b)
-
-    wide = 512 if outs % 512 == 0 else outs
 
     def add_weight(chip):
         for core in range(2):
@@ -316,23 +333,25 @@
     lax.fori_loop(0, hops, sent_pieces, 0)
 
 
-def run_exchange(nb, grad_pre, columns, weight, bias, gamma):
-    rows, outs = grad_pre.shape
+def run_exchange(nb, x_first, pre_act, cotangent, gamma, columns, weight):
+    rows, outs = x_first.shape
     cols = weight.shape[1]
     nc, per, hops = nb // 2, nb // 2, nb // 4
-    parts = 4 if rows % 64 == 0 else 1
+    parts = 8 if rows % 128 == 0 else 4 if rows % 64 == 0 else 1
     dma = pltpu.SemaphoreType.DMA
     vmem = pl.BlockSpec(memory_space=pltpu.VMEM)
     return pl.pallas_call(
         functools.partial(exchange, nb, parts),
         out_shape=(
+            jax.ShapeDtypeStruct((rows, outs), BF16),
             jax.ShapeDtypeStruct((outs, cols), F32),
             jax.ShapeDtypeStruct(columns.shape, BF16),
             jax.ShapeDtypeStruct((2, outs), F32),
         ),
-        in_specs=[vmem, vmem, pl.BlockSpec(memory_space=pl.ANY), vmem, vmem],
-        out_specs=(vmem, vmem, vmem),
+        in_specs=[vmem] * 5 + [pl.BlockSpec(memory_space=pl.ANY)],
+        out_specs=(vmem,) * 4,
         scratch_shapes=[
+            pltpu.VMEM((rows, outs), BF16),
             pltpu.VMEM((nc, 2 * rows, outs), BF16),
             pltpu.VMEM((nc, 2 * rows, cols), BF16),
             pltpu.VMEM((nc, rows, cols), F32),
@@ -367,28 +386,20 @@
         compiler_params=pltpu.CompilerParams(
             collective_id=0, has_side_effects=True, vmem_limit_bytes=60 * 1024 * 1024
         ),
-    )(grad_pre, columns, weight, bias, gamma)
+    )(x_first, pre_act, cotangent, gamma, columns, weight)
 
 
 def shards(nb, x_first, x_layer, pre_act, gamma, weight, cotangent):
-    pre_full = pre_act.astype(F32)
-    gate_tanh = jnp.tanh(gamma[None, :] * pre_full)
-    hidden = pre_full * gate_tanh
-    cot_full = cotangent.astype(F32)
-    grad_hidden = cot_full * x_first.astype(F32)
-    grad_first = (cot_full * hidden).astype(BF16)
-    slope = 1.0 - gate_tanh * gate_tanh
-    grad_pre = (grad_hidden * (gate_tanh + gamma[None, :] * pre_full * slope)).astype(BF16)
-    local_gamma = jnp.sum(grad_hidden * pre_full * pre_full * slope, axis=0)
-    local_bias = jnp.sum(grad_pre.astype(F32), axis=0)
     rows = x_layer.shape[0]
     per, cols = nb // 2, weight.shape[1]
     aligned = cols % 128 == 0
     columns = x_layer if aligned else x_layer.reshape(rows, per, cols).transpose(1, 0, 2)
-    grad_weight, share, total = run_exchange(nb, grad_pre, columns, weight, local_bias[None], local_gamma[None])
+    grad_first, grad_weight, share, total = run_exchange(
+        nb, x_first, pre_act, cotangent, gamma[None], columns, weight
+    )
     if not aligned:
         share = share.transpose(1, 0, 2).reshape(rows, per * cols)
-    grad_layer = (cot_full + share.astype(F32)).astype(BF16)
+    grad_layer = (cotangent.astype(F32) + share.astype(F32)).astype(BF16)
     return (grad_first, grad_layer, grad_weight, total[0], total[1])
 
 

time: 98.6 us -> 96.5 us (0.979)
  other arithmetic: 5.58 us -> 1.96 us
  Pallas kernels: 87.6 us -> 88.9 us
    reduce_sum x1 -> x0, other arithmetic: 3.62 us -> none  [shards(): local_bias = jnp.sum(grad_pre.astype(F32), axis=0)]
    pallas_call x1, Pallas kernels: 87.6 us -> 88.9 us  [run_exchange(): pl.pallas_call(functools.partial(exchange, nb, parts), out_shape=(jax.Sha...]
    unnamed x3 -> x6, local copies, waits for them, and re-layouts: 3.05 us -> 3.21 us
where the time goes in v4:
time: 96.5 us; the launch traced here: 96.3 us
  Pallas kernels  88.9 us (92%)
  local copies, waits for them, and re-layouts  4.7 us (5%)
  other arithmetic  1.96 us (2%)
    pallas_call x1, Pallas kernels, run_exchange(): pl.pallas_call(functools.partial(exchange, nb, parts), out_shape=(jax.Sha...  88.9 us
    unnamed x6, local copies, waits for them, and re-layouts  3.21 us
    convert_element_type x1, other arithmetic, shards(): grad_layer = (cotangent.astype(F32) + share.astype(F32)).astype(BF16)  1.96 us

profile of v4, /device:TPU:14, one launch (start us, length us, event | category | flops | bytes accessed | tf_op | source)
XLA Modules:
  0.0 96.3 jit_solution(15157914418520278301)
XLA Ops:
  0.6 0.0 copy-start.1
  0.6 88.9 %shard_map.101 = (bf16[128,2048]{1,0:T(8,128)(2,1)}, f32[2048,256]{1,0:T(8,128)}, bf16[128,2048]{1,0:T(8,128)(2,1)}, f32[2,2048]{1,0:T(2,128)}) custom-call(bf16[128,2048]{1,0:T(8,128)(2,1)} %x_ref.1, bf16[128,2048]{1,0:T(8,128)(2,1)} %act_ref.1, bf16[128,2048]{1,0:T(8,128)(2,1)} %cot_ref.1, f32[1,2048]{1,0:T(1,128)} %bitcast.3, bf16[128,2048]{1,0:T(8,128)(2,1)} %cols_ref.1, ...), custom_call_target="tpu_custom_call" | custom-call | tf_op jit(solution)/shard_map/pallas_call | solution.py:343
  89.6 0.0 copy-start
  89.6 1.5 %fusion = (f32[1,2048]{1,0:T(1,128)}, f32[1,2048]{1,0:T(1,128)}) fusion(f32[2,2048]{1,0:T(2,128)} %get-tuple-element.12), kind=kLoop, calls=%fused_computation.1 | loop fusion | bytes 32768 | tf_op jit(solution)/shard_map/slice | solution.py:403
  91.1 0.0 copy-done.1
  91.1 2.0 %add_convert_fusion = bf16[128,2048]{1,0:T(8,128)(2,1)} fusion(bf16[128,2048]{1,0:T(8,128)(2,1)} %get-tuple-element.10, bf16[128,2048]{1,0:T(8,128)(2,1)S(1)} %copy-done.1), kind=kLoop, calls=%fused_computation | loop fusion | flops 1048576 | bytes 1572864 | tf_op jit(solution)/shard_map/convert_element_type | solution.py:402
  93.1 1.9 %copy.13 = bf16[128,2048]{1,0:T(8,128)(2,1)} copy(bf16[128,2048]{1,0:T(8,128)(2,1)} %get-tuple-element.20) | data formatting | bytes 1048576
  94.9 0.0 copy-done
  94.9 1.3 %copy.14 = f32[2048,256]{1,0:T(8,128)} copy(f32[2048,256]{1,0:T(8,128)S(1)} %copy-done) | data formatting | bytes 4194304
Async XLA Ops:
  0.6 90.5 %copy-start.1 = (bf16[128,2048]{1,0:T(8,128)(2,1)S(1)}, bf16[128,2048]{1,0:T(8,128)(2,1)}, u32[]{:S(2)}) copy-start(bf16[128,2048]{1,0:T(8,128)(2,1)} %cot_ref.1) | copy-start | bytes 1572868
  89.6 5.4 %copy-start = (f32[2048,256]{1,0:T(8,128)S(1)}, f32[2048,256]{1,0:T(8,128)}, u32[]{:S(2)}) copy-start(f32[2048,256]{1,0:T(8,128)} %get-tuple-element.22) | copy-start | bytes 6291460

commit v5 on v4

--- a/solution.py
+++ b/solution.py
@@ -253,12 +253,16 @@
         def _():
             each(k - 1, pass_sum)
 
-        each(k, add_weight)
+        @pl.when(k < hops - 1)
+        def _():
+            each(k, add_weight)
+
         return carry
 
     lax.fori_loop(0, hops, hop, 0)
     each(hops, give_sum)
     each(hops - 1, pass_sum)
+    each(hops - 1, add_weight)
     each(hops, add_weight)
     each(hops, pass_sum)
 

time: 96.5 us -> 96.8 us (level)
  no operation moved by 1% of the time
where the time goes in v5:
time: 96.8 us; the launch traced here: 96.5 us
  Pallas kernels  89.2 us (92%)
  local copies, waits for them, and re-layouts  4.7 us (5%)
  other arithmetic  1.96 us (2%)
    pallas_call x1, Pallas kernels, run_exchange(): pl.pallas_call(functools.partial(exchange, nb, parts), out_shape=(jax.Sha...  89.2 us
    unnamed x6, local copies, waits for them, and re-layouts  3.21 us
    convert_element_type x1, other arithmetic, shards(): grad_layer = (cotangent.astype(F32) + share.astype(F32)).astype(BF16)  1.96 us

profile of v5, /device:TPU:14, one launch (start us, length us, event | category | flops | bytes accessed | tf_op | source)
XLA Modules:
  0.0 96.5 jit_solution(10527500737995577380)
XLA Ops:
  0.6 0.0 copy-start.1
  0.6 89.2 %shard_map.101 = (bf16[128,2048]{1,0:T(8,128)(2,1)}, f32[2048,256]{1,0:T(8,128)}, bf16[128,2048]{1,0:T(8,128)(2,1)}, f32[2,2048]{1,0:T(2,128)}) custom-call(bf16[128,2048]{1,0:T(8,128)(2,1)} %x_ref.1, bf16[128,2048]{1,0:T(8,128)(2,1)} %act_ref.1, bf16[128,2048]{1,0:T(8,128)(2,1)} %cot_ref.1, f32[1,2048]{1,0:T(1,128)} %bitcast.3, bf16[128,2048]{1,0:T(8,128)(2,1)} %cols_ref.1, ...), custom_call_target="tpu_custom_call" | custom-call | tf_op jit(solution)/shard_map/pallas_call | solution.py:347
  89.9 0.0 copy-start
  89.9 1.5 %fusion = (f32[1,2048]{1,0:T(1,128)}, f32[1,2048]{1,0:T(1,128)}) fusion(f32[2,2048]{1,0:T(2,128)} %get-tuple-element.12), kind=kLoop, calls=%fused_computation.1 | loop fusion | bytes 32768 | tf_op jit(solution)/shard_map/slice | solution.py:407
  91.4 0.0 copy-done.1
  91.4 2.0 %add_convert_fusion = bf16[128,2048]{1,0:T(8,128)(2,1)} fusion(bf16[128,2048]{1,0:T(8,128)(2,1)} %get-tuple-element.10, bf16[128,2048]{1,0:T(8,128)(2,1)S(1)} %copy-done.1), kind=kLoop, calls=%fused_computation | loop fusion | flops 1048576 | bytes 1572864 | tf_op jit(solution)/shard_map/convert_element_type | solution.py:406
  93.3 1.9 %copy.13 = bf16[128,2048]{1,0:T(8,128)(2,1)} copy(bf16[128,2048]{1,0:T(8,128)(2,1)} %get-tuple-element.20) | data formatting | bytes 1048576
  95.2 0.0 copy-done
  95.2 1.3 %copy.14 = f32[2048,256]{1,0:T(8,128)} copy(f32[2048,256]{1,0:T(8,128)S(1)} %copy-done) | data formatting | bytes 4194304
Async XLA Ops:
  0.6 90.7 %copy-start.1 = (bf16[128,2048]{1,0:T(8,128)(2,1)S(1)}, bf16[128,2048]{1,0:T(8,128)(2,1)}, u32[]{:S(2)}) copy-start(bf16[128,2048]{1,0:T(8,128)(2,1)} %cot_ref.1) | copy-start | bytes 1572868
  89.9 5.4 %copy-start = (f32[2048,256]{1,0:T(8,128)S(1)}, f32[2048,256]{1,0:T(8,128)}, u32[]{:S(2)}) copy-start(f32[2048,256]{1,0:T(8,128)} %get-tuple-element.22) | copy-start | bytes 6291460
